TPU v7x, 32 devices: a whole 2x2x4 slice. The times are simulated.
32 devices in a mesh: groups: 2 (over y), dp: 4 (over x, core), tensor: 4 (over z).
Axes of the slice: x: 2, y: 2, z: 4, core: 2. Of those that a mesh axis runs over, the one named last changes fastest.
Arguments:
- query: bfloat16 [4096, 512], P(('groups', 'dp'), 'tensor'), parts along dimension 0, may hold values from -4.5 to 4.5
- keys: bfloat16 [4096, 512], P(('groups', 'dp'), 'tensor'), parts along dimension 0, may hold values from -4.5 to 4.5
- values: bfloat16 [4096, 512], P(('groups', 'dp'), 'tensor'), parts along dimension 0, may hold values from -6 to 6
- upstream: bfloat16 [4096, 8192], P(('groups', 'dp', 'tensor')), parts along dimension 0, may hold values from -6 to 6
- projection: bfloat16 [512, 8192], P('tensor', 'dp'), may hold values from -0.0625 to 0.0625
- lengths: int32 [8, 8], P(('groups', 'dp')), parts along dimension 0, may hold values from 1 to 256, 512 in all within a row
Outputs:
- grad_query: bfloat16 [4096, 512], P(('groups', 'dp'), 'tensor'), parts along dimension 0
- grad_keys: bfloat16 [4096, 512], P(('groups', 'dp'), 'tensor'), parts along dimension 0
- grad_values: bfloat16 [4096, 512], P(('groups', 'dp'), 'tensor'), parts along dimension 0
- grad_projection: float32 [1024, 8192], P(('groups', 'tensor'), 'dp'), parts along dimension 0
There are 2 independent parts, one for each index of `groups`. A program takes and returns all parts, laid end to end along the dimension named above; an argument that names none is the same for every part. Nothing has to cross between parts.
Inputs may be any that keep to these rules, and one draw needn't show every extreme that they name: Each row holds the lengths of the 8 documents of one sequence in order; they sum to 512 and the largest is exactly 256.
All inputs are finite; a program needn't handle non-finite values.
Results may differ from a plain program's by a relative error of at most 0.014.
Values may be sent and summed in bfloat16 or wider, within the bound.
No kernel may reach another device: no remote copies, remote signals or barrier semaphores. Data moves between devices by JAX's collectives and lax.ppermute only.
A program may use at most 64 MiB of HBM per device.

v0:
```python
import jax
import jax.numpy as jnp
from jax import lax
from jax.sharding import PartitionSpec as P

HD = 128


def sequence_mask(length_row, row_count):
    segment_ends = jnp.cumsum(length_row)
    places = jnp.arange(row_count, dtype=jnp.int32)
    labels = jnp.sum((segment_ends[None, :] <= places[:, None]).astype(jnp.int32), axis=1)
    same = labels[:, None] == labels[None, :]
    return jnp.logical_and(same, places[None, :] <= places[:, None])


def shards(query, keys, values, upstream, projection, lengths):
    row_count, width = query.shape
    head_count = width // HD
    scaling = HD ** (-0.5)
    allowed = sequence_mask(lengths[0], row_count)
    query_heads = query.reshape(row_count, head_count, HD)
    key_heads = keys.reshape(row_count, head_count, HD)
    value_heads = values.reshape(row_count, head_count, HD)
    scores = (
        jnp.einsum("qhd,khd->hqk", query_heads, key_heads, preferred_element_type=jnp.float32)
        * scaling
    )
    scores = jnp.where(allowed[None], scores, -1e30)
    row_max = jnp.max(scores, axis=2, keepdims=True)
    exponent = jnp.exp(scores - row_max)
    probs = exponent / jnp.sum(exponent, axis=2, keepdims=True)
    probs_low = probs.astype(jnp.bfloat16)
    attended = jnp.einsum(
        "hqk,khd->qhd", probs_low, value_heads, preferred_element_type=jnp.float32
    )
    attended = attended.astype(jnp.bfloat16).reshape(row_count, width)
    full_projection = lax.all_gather(projection, "dp", axis=1, tiled=True)
    gathered = lax.all_gather(upstream, "tensor", axis=0, tiled=True)
    out_total = lax.dot_general(
        gathered, full_projection, (((1,), (1,)), ((), ())), preferred_element_type=jnp.float32
    )
    partial_grad = lax.dot_general(
        attended, gathered, (((0,), (0,)), ((), ())), preferred_element_type=jnp.float32
    )
    grad_projection = lax.psum_scatter(
        partial_grad.astype(jnp.bfloat16), "dp", scatter_dimension=1, tiled=True
    ).astype(jnp.float32)
    out_grad = out_total.astype(jnp.bfloat16)
    grad_heads = out_grad.reshape(row_count, head_count, HD)
    grad_values = jnp.einsum(
        "hqk,qhd->khd", probs_low, grad_heads, preferred_element_type=jnp.float32
    ).astype(jnp.bfloat16)
    grad_probs = jnp.einsum(
        "qhd,khd->hqk", grad_heads, value_heads, preferred_element_type=jnp.float32
    )
    delta = jnp.sum(probs * grad_probs, axis=2, keepdims=True)
    grad_scores = (probs * (grad_probs - delta) * scaling).astype(jnp.bfloat16)
    grad_query = jnp.einsum(
        "hqk,khd->qhd", grad_scores, key_heads, preferred_element_type=jnp.float32
    ).astype(jnp.bfloat16)
    grad_keys = jnp.einsum(
        "hqk,qhd->khd", grad_scores, query_heads, preferred_element_type=jnp.float32
    ).astype(jnp.bfloat16)
    return (
        grad_query.reshape(row_count, width),
        grad_keys.reshape(row_count, width),
        grad_values.reshape(row_count, width),
        grad_projection,
    )


def solution(mesh):
    in_specs = (
        P(("groups", "dp"), "tensor"),
        P(("groups", "dp"), "tensor"),
        P(("groups", "dp"), "tensor"),
        P(("groups", "dp", "tensor"), None),
        P("tensor", "dp"),
        P(("groups", "dp"), None),
    )
    out_specs = (
        P(("groups", "dp"), "tensor"),
        P(("groups", "dp"), "tensor"),
        P(("groups", "dp"), "tensor"),
        P(("groups", "tensor"), "dp"),
    )
    return jax.shard_map(shards, mesh=mesh, in_specs=in_specs, out_specs=out_specs, check_vma=False)
```

profile of v0, /device:TPU:0, one launch (start us, length us, event | category | flops | bytes accessed | tf_op | source)
XLA Modules:
  0.0 226.7 jit_solution(17024745603641305551)
XLA Ops:
  7.2 0.0 copy-start
  7.2 0.0 all-gather.3.cloned.1.call-start
  7.2 0.7 all-gather.3.cloned.1.call-update
  7.9 0.0 all-gather.5.cloned.1.call-start
  8.0 0.7 all-gather.5.cloned.1.call-update
  8.7 0.0 reduce-scatter.2.cloned.1.call-start
  8.7 0.8 reduce-window.8
  9.5 0.1 convert_reduce_fusion
  9.6 1.3 fusion.11
  10.9 0.2 fusion.4
  11.1 150.8 %all-gather.3.cloned.1.call-done = bf16[512,8192]{1,0:T(8,128)(2,1)} async-done(((bf16[128,8192]{1,0:T(8,128)(2,1)}), bf16[512,8192]{1,0:T(8,128)(2,1)}) %all-gather.3.cloned.1.call-update) | async-done | bytes 8388624 | tf_op jit(solution)/shard_map/all_gather | solution.py:39
  161.9 0.0 copy-done
  161.9 6.5 %convolution_convert_fusion = bf16[128,8192]{1,0:T(8,128)(2,1)} fusion(bf16[512,8192]{1,0:T(8,128)(2,1)} %all-gather.3.cloned.1.call-done, bf16[512,128]{1,0:T(8,128)(2,1)S(1)} %copy-done, f32[512,512]{0,1:T(8,128)S(1)} %get-tuple-element.13, f32[512]{0:T(512)S(1)} %fusion.4, f32[512]{0:T(512)S(1)} %get-tuple-element.12), kind=kOutput, calls=%fused_computation | convolution fusion | flops 1142751232 | bytes 11669504 | tf_op jit(solution)/shard_map/dot_general | solution.py:43
  168.4 0.0 reduce-scatter.2.cloned.1.call-update
  168.4 15.8 %all-gather.5.cloned.1.call-done = bf16[128,8192]{1,0:T(8,128)(2,1)} async-done(((bf16[128,2048]{1,0:T(8,128)(2,1)}), bf16[128,8192]{1,0:T(8,128)(2,1)}) %all-gather.5.cloned.1.call-update) | async-done | bytes 2097168 | tf_op jit(solution)/shard_map/all_gather | solution.py:38
  184.3 6.3 %convolution_convert_fusion.5 = bf16[512,128]{1,0:T(8,128)(2,1)S(1)} fusion(bf16[512,8192]{1,0:T(8,128)(2,1)} %all-gather.3.cloned.1.call-done, bf16[128,8192]{1,0:T(8,128)(2,1)} %all-gather.5.cloned.1.call-done), kind=kOutput, calls=%fused_computation.7 | convolution fusion | flops 1073807360 | bytes 10616832 | tf_op jit(solution)/shard_map/dot_general | solution.py:40
  190.6 0.3 fusion.1
  190.9 0.0 copy-start.1
  190.9 0.0 copy-start.2
  191.0 0.8 copy.11
  191.7 0.3 multiply_reduce_fusion
  192.0 0.3 multiply_convert_fusion
  192.3 0.0 copy-done.1
  192.3 1.0 convolution_convert_fusion.3
  193.3 0.0 copy-done.2
  193.3 1.0 convolution_convert_fusion.4
  194.3 23.7 %reduce-scatter.2.cloned.1.call-done = bf16[128,2048]{1,0:T(8,128)(2,1)} async-done(((bf16[128,8192]{1,0:T(8,128)(2,1)}), bf16[128,2048]{1,0:T(8,128)(2,1)}) %reduce-scatter.2.cloned.1.call-update) | async-done | bytes 524304 | tf_op jit(solution)/shard_map/reduce_scatter | solution.py:46
  218.0 2.1 convert_element_type.58
Async XLA Ops:
  7.2 154.8 %copy-start = (bf16[512,128]{1,0:T(8,128)(2,1)S(1)}, bf16[512,128]{1,0:T(8,128)(2,1)}, u32[]{:S(2)}) copy-start(bf16[512,128]{1,0:T(8,128)(2,1)} %param.8) | copy-start | bytes 393220
  7.2 154.7 %all-gather.3.cloned.1.call-start = ((), (), s32[]{:S(2)}) async-start(), calls=%async_computation.1 | async-start | bytes 10485760 | tf_op jit(solution)/shard_map/all_gather | solution.py:39
  7.9 176.4 %all-gather.5.cloned.1.call-start = ((), (), s32[]{:S(2)}) async-start(), calls=%async_computation.2 | async-start | bytes 2621440 | tf_op jit(solution)/shard_map/all_gather | solution.py:38
  8.7 209.3 %reduce-scatter.2.cloned.1.call-start = ((), (), s32[]{:S(2)}) async-start(), calls=%async_computation.3 | async-start | bytes 2621440 | tf_op jit(solution)/shard_map/reduce_scatter | solution.py:46
  190.9 1.4 copy-start.1
  190.9 2.4 %copy-start.2 = (bf16[512,128]{1,0:T(8,128)(2,1)S(1)}, bf16[512,128]{1,0:T(8,128)(2,1)}, u32[]{:S(2)}) copy-start(bf16[512,128]{1,0:T(8,128)(2,1)} %param.7) | copy-start | bytes 393220
Sparse Core Ops, SparseCore 0:
  9.6 152.3 all-gather.2
  163.5 20.7 all-gather.4
  186.8 31.1 reduce-scatter.1
where the time goes:
time: 227 us
  waiting for transfers between devices  192 us (85%)
  matrix products  16.7 us (7%)
  between operations  13.8 us (6%)
  other arithmetic  3.53 us (2%)
    all_gather x1, waiting for transfers between devices, shards(): gathered = lax.all_gather(upstream, 'tensor', axis=0, tiled=True)  151 us
    reduce_scatter x1, waiting for transfers between devices, shards(): lax.psum_scatter(partial_grad.astype(jnp.bfloat16), 'dp', scatter_dimensi...  23.7 us
    all_gather x1, waiting for transfers between devices, shards(): full_projection = lax.all_gather(projection, 'dp', axis=1, tiled=True)  15.8 us
    dot_general x1, matrix products, shards(): lax.dot_general(attended, gathered, (((0,), (0,)), ((), ())), preferred_e...  6.48 us
    dot_general x1, matrix products, shards(): lax.dot_general(gathered, full_projection, (((1,), (1,)), ((), ())), pref...  6.31 us
  transfers between devices with their start and end apart: 3, of which 3 were waited for; matrix products, arithmetic and copies ran while one was open for 8% of the time, Pallas kernels for 0%

commit v1 on v0

--- a/solution.py
+++ b/solution.py
@@ -36,7 +36,12 @@
     )
     attended = attended.astype(jnp.bfloat16).reshape(row_count, width)
     full_projection = lax.all_gather(projection, "dp", axis=1, tiled=True)
-    gathered = lax.all_gather(upstream, "tensor", axis=0, tiled=True)
+
+    def try_all_sums_all(local_x, where_dim):
+        aux = jax.lax.all_to_all(jnp.stack([local_x] * jax.lax.axis_size("tensor")), "tensor", 0, 0)
+        return jnp.concatenate(aux, axis=where_dim)
+
+    gathered = try_all_sums_all(upstream, where_dim=0)
     out_total = lax.dot_general(
         gathered, full_projection, (((1,), (1,)), ((), ())), preferred_element_type=jnp.float32
     )

time: 227 us -> 250 us (1.10)
  waiting for transfers between devices: 192 us -> 204 us
  starting transfers between devices: 0.11 us -> 6.52 us
  local copies, waits for them, and re-layouts: 0.78 us -> 6.63 us
    all_to_all x0 -> x1, waiting for transfers between devices: none -> 182 us  [try_all_sums_all(): jax.lax.all_to_all(jnp.stack([local_x] * jax.lax.axis_size('tensor')), 't...]
    all_gather x1 -> x0, waiting for transfers between devices: 151 us -> none  [shards(): gathered = lax.all_gather(upstream, 'tensor', axis=0, tiled=True)]
    all_gather x1, waiting for transfers between devices: 15.8 us -> 0.02 us  [shards(): full_projection = lax.all_gather(projection, 'dp', axis=1, tiled=True)]
    all_to_all x0 -> x1, starting transfers between devices: none -> 6.48 us  [try_all_sums_all(): jax.lax.all_to_all(jnp.stack([local_x] * jax.lax.axis_size('tensor')), 't...]
    another operation x0 -> x1, local copies, waits for them, and re-layouts: none -> 5.85 us  [try_all_sums_all(): jnp.stack([local_x] * jax.lax.axis_size('tensor'))]
    reduce_scatter x1, waiting for transfers between devices: 23.7 us -> 20.5 us  [shards(): lax.psum_scatter(partial_grad.astype(jnp.bfloat16), 'dp', scatter_dimensi...]
  transfers between devices with their start and end apart: 3 -> 3, of which waited for: 3 -> 2; matrix products, arithmetic and copies ran while one was open for 8% -> 7% of each run, Pallas kernels for 0% -> 0%
where the time goes in v1:
time: 250 us
  waiting for transfers between devices  204 us (82%)
  matrix products  15.9 us (6%)
  between operations  14.1 us (6%)
  local copies, waits for them, and re-layouts  6.63 us (3%)
  starting transfers between devices  6.52 us (3%)
  other arithmetic  2.87 us (1%)
    all_to_all x1, waiting for transfers between devices, try_all_sums_all(): jax.lax.all_to_all(jnp.stack([local_x] * jax.lax.axis_size('tensor')), 't...  182 us
    reduce_scatter x1, waiting for transfers between devices, shards(): lax.psum_scatter(partial_grad.astype(jnp.bfloat16), 'dp', scatter_dimensi...  20.5 us
    dot_general x1, matrix products, shards(): lax.dot_general(attended, gathered, (((0,), (0,)), ((), ())), preferred_e...  6.57 us
    all_to_all x1, starting transfers between devices, try_all_sums_all(): jax.lax.all_to_all(jnp.stack([local_x] * jax.lax.axis_size('tensor')), 't...  6.48 us
    dot_general x1, matrix products, shards(): lax.dot_general(gathered, full_projection, (((1,), (1,)), ((), ())), pref...  6.31 us
    another operation x1, local copies, waits for them, and re-layouts, try_all_sums_all(): jnp.stack([local_x] * jax.lax.axis_size('tensor'))  5.85 us
  transfers between devices with their start and end apart: 3, of which 2 were waited for; matrix products, arithmetic and copies ran while one was open for 7% of the time, Pallas kernels for 0%

profile of v1, /device:TPU:0, one launch (start us, length us, event | category | flops | bytes accessed | tf_op | source)
XLA Modules:
  0.0 249.7 jit_solution(6975570248987011440)
XLA Ops:
  7.2 0.0 copy-start
  7.2 5.9 %stack.2 = bf16[4,128,8192]{2,1,0:T(8,128)(2,1)} broadcast(bf16[128,8192]{1,0:T(8,128)(2,1)} %param.9), dimensions={1,2} | broadcast | bytes 10485760 | tf_op jit(solution)/shard_map/stack | solution.py:41
  13.0 0.0 copy-start.3
  13.0 0.0 copy-start.1
  13.0 0.0 copy-start.2
  13.0 6.5 %all-to-all-start = ((bf16[4,128,8192]{2,1,0:T(8,128)(2,1)}), bf16[4,128,8192]{2,1,0:T(8,128)(2,1)}, u32[]{:S(2)}, u32[]{:S(2)}) async-start(bf16[4,128,8192]{2,1,0:T(8,128)(2,1)} %stack.2), calls=%async_computation | async-start | bytes 16777216 | tf_op jit(solution)/shard_map/all_to_all | solution.py:41
  19.5 0.0 all-gather.2.cloned.1.call-start
  19.5 0.7 all-gather.2.cloned.1.call-update
  20.2 0.0 reduce-scatter.2.cloned.1.call-start
  20.3 0.0 copy-done.3
  20.3 0.2 reduce-window.8
  20.5 0.1 convert_reduce_fusion
  20.6 0.0 copy-done.1
  20.6 0.0 copy-done.2
  20.6 0.4 fusion.11
  20.9 0.2 fusion.4
  21.1 182.5 %all-to-all-done = bf16[4,128,8192]{2,1,0:T(8,128)(2,1)} async-done(((bf16[4,128,8192]{2,1,0:T(8,128)(2,1)}), bf16[4,128,8192]{2,1,0:T(8,128)(2,1)}, u32[]{:S(2)}, u32[]{:S(2)}) %all-to-all-start) | async-done | bytes 8388640 | tf_op jit(solution)/shard_map/all_to_all | solution.py:41
  203.6 0.0 copy-done
  203.6 6.6 %convolution_convert_fusion = bf16[128,8192]{1,0:T(8,128)(2,1)} fusion(bf16[512,8192]{1,0:T(8,128)(2,1)} %bitcast.2, bf16[512,128]{1,0:T(8,128)(2,1)S(1)} %copy-done, f32[512,512]{0,1:T(8,128)S(1)} %get-tuple-element.13, f32[512]{0:T(512)S(1)} %fusion.4, f32[512]{0:T(512)S(1)} %get-tuple-element.12), kind=kOutput, calls=%fused_computation | convolution fusion | flops 1142751232 | bytes 11669504 | tf_op jit(solution)/shard_map/dot_general | solution.py:48
  210.2 0.0 reduce-scatter.2.cloned.1.call-update
  210.2 0.0 all-gather.2.cloned.1.call-done
  210.2 6.3 %convolution_convert_fusion.5 = bf16[512,128]{1,0:T(8,128)(2,1)S(1)} fusion(bf16[512,8192]{1,0:T(8,128)(2,1)} %bitcast.2, bf16[128,8192]{1,0:T(8,128)(2,1)} %all-gather.2.cloned.1.call-done), kind=kOutput, calls=%fused_computation.7 | convolution fusion | flops 1073807360 | bytes 10616832 | tf_op jit(solution)/shard_map/dot_general | solution.py:45
  216.6 0.3 fusion.1
  216.9 0.8 copy.11
  217.7 0.3 multiply_reduce_fusion
  218.0 0.3 multiply_convert_fusion
  218.3 1.0 convolution_convert_fusion.3
  219.2 1.0 convolution_convert_fusion.4
  220.2 20.5 %reduce-scatter.2.cloned.1.call-done = bf16[128,2048]{1,0:T(8,128)(2,1)} async-done(((bf16[128,8192]{1,0:T(8,128)(2,1)}), bf16[128,2048]{1,0:T(8,128)(2,1)}) %reduce-scatter.2.cloned.1.call-update) | async-done | bytes 524304 | tf_op jit(solution)/shard_map/reduce_scatter | solution.py:51
  240.7 2.1 convert_element_type.58
Async XLA Ops:
  7.2 196.4 %copy-start = (bf16[512,128]{1,0:T(8,128)(2,1)S(1)}, bf16[512,128]{1,0:T(8,128)(2,1)}, u32[]{:S(2)}) copy-start(bf16[512,128]{1,0:T(8,128)(2,1)} %param.8) | copy-start | bytes 393220
  13.0 7.3 %copy-start.3 = (s32[1,8]{1,0:T(1,128)S(1)}, s32[1,8]{1,0:T(1,128)}, u32[]{:S(2)}) copy-start(s32[1,8]{1,0:T(1,128)} %param.11) | copy-start | bytes 100
  13.0 7.5 %copy-start.1 = (bf16[512,128]{1,0:T(8,128)(2,1)S(1)}, bf16[512,128]{1,0:T(8,128)(2,1)}, u32[]{:S(2)}) copy-start(bf16[512,128]{1,0:T(8,128)(2,1)} %param.6) | copy-start | bytes 393220
  13.0 7.5 %copy-start.2 = (bf16[512,128]{1,0:T(8,128)(2,1)S(1)}, bf16[512,128]{1,0:T(8,128)(2,1)}, u32[]{:S(2)}) copy-start(bf16[512,128]{1,0:T(8,128)(2,1)} %param.7) | copy-start | bytes 393220
  13.0 190.6 %all-to-all-start = ((bf16[4,128,8192]{2,1,0:T(8,128)(2,1)}), bf16[4,128,8192]{2,1,0:T(8,128)(2,1)}, u32[]{:S(2)}, u32[]{:S(2)}) async-start(bf16[4,128,8192]{2,1,0:T(8,128)(2,1)} %stack.2), calls=%async_computation | async-start | bytes 16777216 | tf_op jit(solution)/shard_map/all_to_all | solution.py:41
  19.5 190.7 %all-gather.2.cloned.1.call-start = ((), (), s32[]{:S(2)}) async-start(), calls=%async_computation.2 | async-start | bytes 2621440 | tf_op jit(solution)/shard_map/all_gather | solution.py:38
  20.2 220.5 %reduce-scatter.2.cloned.1.call-start = ((), (), s32[]{:S(2)}) async-start(), calls=%async_computation.3 | async-start | bytes 2621440 | tf_op jit(solution)/shard_map/reduce_scatter | solution.py:51
Sparse Core Ops, SparseCore 0:
  21.9 24.7 all-gather.1
  210.3 30.3 reduce-scatter.1
